TPU v7x, 32 devices: a whole 2x2x4 slice. The times are simulated.
32 devices in a mesh: dev: 32 (over z, y, x, core).
Axes of the slice: x: 2, y: 2, z: 4, core: 2. Of those that a mesh axis runs over, the one named last changes fastest.
Arguments:
- features: bfloat16 [16384, 1024], P('dev'), may hold values from -6 to 6
- w_hidden: bfloat16 [1024, 512], replicated, may hold values from -0.1875 to 0.1875
- w_out: bfloat16 [512, 128], replicated, may hold values from -0.25 to 0.25
- items: bfloat16 [65536, 128], P('dev'), may hold values from -200 to 200
- routes: int32 [16384, 4], P('dev'), may hold values from 0 to 511, all different within a row; in each aligned block of 512 rows (0 to 511, 512 to 1023, ...) at most 8 rows name the same one
- cluster_slot: int32 [512], replicated, may hold values from 0 to 511, each once
- sample_ids: int32 [512, 4096], P('dev'), may hold values from 0 to 127
- sample_counts: int32 [512, 4096], P('dev'), may hold values from 1 to 4095
- positives: int32 [16384, 4], P('dev'), may hold values from 0 to 4095
Outputs:
- slot_loss: float32 [512], P('dev')
- grad_hidden: float32 [1024, 512], replicated
- grad_out: float32 [512, 128], replicated
- item_grad: float32 [65536, 128], P('dev')
Inputs may be any that keep to these rules, and one draw needn't show every extreme that they name: `routes`: each row names 4 different clusters; within the rows of one device no cluster is named more than 8 times; every cluster is named by some row. `cluster_slot`: each cluster has one slot.
All inputs are finite; a program needn't handle non-finite values.
Results may differ from a plain program's by a relative error of at most 0.012.
The roundings to bfloat16 on the way count: a program that leaves them out, or rounds other values in their place, can miss the bound.
Values may be sent and summed in bfloat16 or wider, within the bound.
A program may use at most 128 MiB of HBM per device.

v0:
```python
import functools

import jax
import jax.numpy as jnp
from jax import lax
from jax.experimental import pallas as pl
from jax.experimental.pallas import tpu as pltpu
from jax.sharding import PartitionSpec as P

LINE = 4
LANES = 128
TILE = 8
MESH = pl.DeviceIdType.MESH
F32, BF16, I32 = jnp.float32, jnp.bfloat16, jnp.int32
VMEM_BYTES = 48 * 1024 * 1024


def iota(shape, axis):
    return lax.broadcasted_iota(I32, shape, axis)


def flags(test):
    return jnp.where(test, 1.0, 0.0).astype(BF16)


def log2(value):
    return value.bit_length() - 1


def flip(index, other, size):
    result = index
    weight = 1
    while weight < size:
        mine = (index // weight) % 2
        theirs = (other // weight) % 2
        result = result + weight * (theirs - 2 * mine * theirs)
        weight *= 2
    return result


def each(low, high, action):
    def body(i, carry):
        action(i)
        return carry

    lax.fori_loop(low, high, body, 0)


def remote(src, dst, sems, at, device):
    return pltpu.make_async_remote_copy(
        src_ref=src,
        dst_ref=dst,
        send_sem=sems.at[(0,) + at],
        recv_sem=sems.at[(1,) + at],
        device_id=(device,),
        device_id_type=MESH,
    )


def summed_groups(line, chips, elements):
    parts = line * chips * TILE
    units = -(-(elements // LANES) // (2 * parts))
    pieces = 3
    groups = []
    start = 0
    for n in range(pieces):
        plane_first, share = True, (units + pieces - 1 - n) // pieces
        if share > 0:
            groups.append((plane_first, start, share * parts))
            start += share * parts
    return groups, start


def step_kernel(
    line,
    plane,
    cap,
    features_hbm,
    w_hidden_hbm,
    w_out_hbm,
    items_hbm,
    ids_hbm,
    counts_hbm,
    routes_hbm,
    spots_hbm,
    slot_hbm,
    loss_out,
    big_out,
    small_out,
    table_out,
    features,
    features_t,
    w_hidden,
    w_out,
    items,
    ids,
    counts,
    routes_ref,
    spots_ref,
    slot_ref,
    slope,
    hidden,
    metas,
    qline,
    earlier,
    codes,
    sel,
    stage,
    got,
    zstage,
    zgot,
    lookup,
    mass_left,
    mass_right,
    mass_grid,
    mass,
    tpos,
    own_item,
    own_count,
    wts,
    dqs,
    ret,
    pstage,
    part,
    acc,
    outb,
    core_in,
    inboxes,
    full,
    load_sem,
    m_sem,
    q_sem,
    x_sem,
    t_sem,
    r_sem,
    p_sem,
    c_sem,
    s1_sem,
    s2_sem,
    g1_sem,
    g2_sem,
    go_sem,
):
    me = lax.axis_index("dev")
    z, p = me // plane, me % plane

    def along(j):
        return flip(z, j, line) * plane + p

    def inside(i):
        return z * plane + flip(p, i, plane)

    visits, users = routes_ref.shape
    clusters = slot_ref.shape[1]
    local_clusters, samples = ids.shape
    item_rows, width = items.shape[1:]
    rows = local_clusters * cap
    hosted = plane * local_clusters
    seats = line * plane * cap
    groups = samples // LANES

    piece = users // 2
    top, bottom = pl.ds(0, piece), pl.ds(piece, piece)
    loads = [
        pltpu.make_async_copy(src, dst, load_sem.at[n])
        for n, (src, dst) in enumerate(
            [
                (w_hidden_hbm, w_hidden),
                (features_hbm.at[top, :], features.at[top, :]),
                (w_out_hbm, w_out),
                (features_hbm.at[bottom, :], features.at[bottom, :]),
                (routes_hbm, routes_ref),
                (spots_hbm, spots_ref),
                (slot_hbm, slot_ref),
                (ids_hbm, ids),
                (counts_hbm, counts),
                (items_hbm, items),
            ]
        )
    ]
    for load in loads:
        load.start()

    barrier = pltpu.get_barrier_semaphore()
    for j in range(1, line):
        pl.semaphore_signal(barrier, inc=1, device_id=(along(j),), device_id_type=MESH)
    each(
        1,
        plane,
        lambda i: pl.semaphore_signal(
            barrier, inc=1, device_id=(inside(i),), device_id_type=MESH
        ),
    )

    pl.semaphore_wait(barrier, line + plane - 2)

    def meta_copies(j):
        return [
            remote(src, metas.at[n, j], m_sem, (n, j), along(j))
            for n, src in enumerate((routes_ref, spots_ref))
        ]

    def half_copy(stock, arrived, sems, j, h, source, device):
        span = pl.ds(h * piece, piece)
        return remote(stock.at[source, span], arrived.at[j, span], sems, (j, h), device)

    def query_copy(j, h):
        source, device = (2, along(1)) if j == 3 else (0, along(j))
        return half_copy(qline, qline, q_sem, j, h, source, device)

    def seat_copy(j, i):
        return remote(stage.at[j, i], got.at[:, j * plane + i], x_sem, (j, i), inside(i))

    def target_copy(i):
        return remote(zstage.at[i], zgot.at[i], t_sem, (i,), inside(i))

    def back_copy(j, i):
        return remote(dqs.at[:, j * plane + i], ret.at[j, i], r_sem, (j, i), inside(i))

    def part_copy(j, h):
        return half_copy(pstage, part, p_sem, j, h, j, along(1 if j == 3 else j))

    for load in loads[0:3]:
        load.wait()
    for h in range(2):
        if h == 1:
            loads[3].wait()
        span = slice(h * piece, (h + 1) * piece)
        pre = jnp.dot(features[span, :], w_hidden[...], preferred_element_type=F32)
        gate = 1.0 / (1.0 + jnp.exp(-pre))
        active = (pre * gate).astype(BF16)
        hidden[span, :] = active
        slope[span, :] = pre
        qline[0, span, :] = jnp.dot(active, w_out[...], preferred_element_type=F32).astype(BF16)
        query_copy(2, h).start()
        query_copy(1, h).start()

    for load in loads[4:6]:
        load.wait()
    for j in range(1, line):
        for copy in meta_copies(j):
            copy.start()
    earlier[...] = flags(iota((users, users), 0) < iota((users, users), 1))
    loads[6].wait()
    k = iota((hosted, 1), 0)
    host = lax.bitwise_xor(lax.shift_right_logical(k, log2(local_clusters)), p)
    slot = (z * plane + host) * local_clusters + (k & (local_clusters - 1))
    names = jnp.sum(
        jnp.where(slot_ref[...] == slot, iota((hosted, clusters), 1), 0).astype(F32),
        axis=1,
        keepdims=True,
    ).astype(I32)

    lane = iota((1, LANES), 1)
    zstage[...] = jnp.zeros(zstage.shape, F32)

    def choose(j):
        routes = routes_ref if j == 0 else metas.at[0, j]
        spots = spots_ref if j == 0 else metas.at[1, j]
        target = jnp.zeros((hosted, users), F32)
        for r in range(visits):
            same = names == routes[r : r + 1, :]
            target = jnp.where(same, (spots[r : r + 1, :] + 1).astype(F32), target)
        member = target > 0.0
        rank = jnp.dot(flags(member), earlier[...], preferred_element_type=F32)
        code = jnp.where(member, rank, -1.0)
        codes[...] = code
        found = zstage[...].reshape(hosted, LANES)
        for s in range(cap):
            spot = jnp.sum(jnp.where(code == float(s), target, 0.0), axis=1, keepdims=True)
            found = jnp.where(lane == j * cap + s, spot, found)
        zstage[...] = found.reshape(plane, local_clusters, LANES)

        def block(i):
            own = codes[pl.ds(pl.multiple_of(i * local_clusters, TILE), local_clusters), :]
            if cap % TILE == 0:
                seat = iota((1, cap, 1), 1).astype(F32)
                chosen = flags((own[:, None, :] == seat).reshape(rows, users))
            else:
                first = iota((rows, local_clusters), 1) * cap
                row = iota((rows, local_clusters), 0)
                spread = flags((row >= first) & (row < first + cap))
                seat = (iota((rows, 1), 0) & (cap - 1)).astype(F32)
                wide = jnp.dot(spread, own.astype(BF16), preferred_element_type=F32)
                chosen = flags(wide == seat)
            sel[j, i] = chosen

        each(0, plane, block)

    def seated(j, i):
        value = jnp.dot(sel[j, i], qline[j], preferred_element_type=F32)
        return value.reshape(local_clusters, cap, width).astype(BF16)

    def send_seats(j):
        def block(i):
            stage[j, i] = seated(j, i)
            seat_copy(j, i).start()

        each(1, plane, block)
        got[:, j * plane] = seated(j, 0)

    def relay():
        for h in range(2):
            query_copy(2, h).wait_recv()
            query_copy(3, h).start()

    choose(0)
    send_seats(0)
    for j in range(1, line):
        for copy in meta_copies(j):
            copy.wait_recv()
        choose(j)
        if j == 2:
            relay()
    each(1, plane, lambda i: target_copy(i).start())
    zgot[0] = zstage[0]
    for h in range(2):
        query_copy(1, h).wait_recv()
    send_seats(1)
    send_seats(2)

    for load in loads[7:]:
        load.wait()
    for t in range(groups):
        here = slice(t * LANES, (t + 1) * LANES)
        count = counts[:, here]
        high = lax.shift_right_logical(count, 6)
        lookup[:, t, :] = ids[:, here].astype(F32)
        lookup[:, groups + t, :] = high.astype(F32)
        lookup[:, 2 * groups + t, :] = (count & 63).astype(F32)

    digit = 16
    tall = item_rows // digit
    chunk = mass_left.shape[1]
    mass_grid[...] = jnp.zeros(mass_grid.shape, F32)

    def weigh(t):
        here = pl.ds(pl.multiple_of(t * chunk, LANES), chunk)
        rest = 1.0 / counts[:, here].astype(F32)
        terms = []
        for _ in range(3):
            term = rest.astype(BF16).astype(F32)
            rest = rest - term
            terms.append(term)
        high = lax.shift_right_logical(ids[:, here], log2(digit))
        low = ids[:, here] & (digit - 1)
        for c in range(local_clusters):
            match = high[c : c + 1, :] == iota((tall, chunk), 0)
            mass_left[c * 3 * tall : (c + 1) * 3 * tall, :] = jnp.concatenate(
                [jnp.where(match, term[c : c + 1, :], 0.0) for term in terms], axis=0
            ).astype(BF16)
            mass_right[c * digit : (c + 1) * digit, :] = flags(
                low[c : c + 1, :] == iota((digit, chunk), 0)
            )
        mass_grid[...] += lax.dot_general(
            mass_left[...],
            mass_right[...],
            (((1,), (1,)), ((), ())),
            preferred_element_type=F32,
        )

    def settle_masses():
        across = local_clusters * digit
        column = iota((tall, across), 1)
        grid = jnp.zeros((tall, across), F32)
        for c in range(local_clusters):
            rows_c = mass_grid[c * 3 * tall : (c + 1) * 3 * tall, :]
            block = rows_c[0:tall] + rows_c[tall : 2 * tall] + rows_c[2 * tall : 3 * tall]
            grid = jnp.where(lax.shift_right_logical(column, log2(digit)) == c, block, grid)
        item = iota((item_rows, tall), 0)
        rise = jnp.where(
            lax.shift_right_logical(item, log2(digit)) == iota((item_rows, tall), 1), 1.0, 0.0
        )
        exact = lax.Precision.HIGHEST
        wide = jnp.dot(rise, grid, preferred_element_type=F32, precision=exact)
        same = (iota((item_rows, across), 0) & (digit - 1)) == (
            iota((item_rows, across), 1) & (digit - 1)
        )
        pick = jnp.where(
            lax.shift_right_logical(iota((across, local_clusters), 0), log2(digit))
            == iota((across, local_clusters), 1),
            1.0,
            0.0,
        )
        logs = jnp.log(
            jnp.dot(
                jnp.where(same, wide, 0.0), pick, preferred_element_type=F32, precision=exact
            )
        )
        for c in range(local_clusters):
            mass[c] = logs[:, c : c + 1]

    chunks = samples // chunk
    each(0, chunks // 2, weigh)
    for h in range(2):
        query_copy(3, h).wait_recv()
    send_seats(3)
    each(chunks // 2, chunks, weigh)
    settle_masses()
    pre = slope[...]
    gate = 1.0 / (1.0 + jnp.exp(-pre))
    slope[...] = gate * (1.0 + pre * (1.0 - gate))

    features_t[...] = features[...].T
    each(1, plane, lambda i: target_copy(i).wait_recv())

    entry = iota((LANES, seats), 0)
    column = iota((LANES, seats), 1)
    source = lax.shift_right_logical(column, log2(cap))
    place = lax.shift_right_logical(source, log2(plane)) * cap + (column & (cap - 1))
    widen = flags(entry == place)
    from_row = lax.shift_right_logical(iota((hosted, seats), 0), log2(local_clusters))
    from_column = lax.shift_right_logical(iota((hosted, seats), 1), log2(cap)) & (plane - 1)
    matched = from_row == from_column
    fold = flags(
        iota((local_clusters, hosted), 0)
        == (iota((local_clusters, hosted), 1) & (local_clusters - 1))
    )
    z_all = zgot[...].reshape(hosted, LANES)
    z_high = jnp.floor(z_all * (1.0 / 64.0))
    z_low = z_all - z_high * 64.0

    def regroup(value):
        spread = jnp.dot(value.astype(BF16), widen, preferred_element_type=F32)
        spread = jnp.where(matched, spread, 0.0).astype(BF16)
        return jnp.dot(fold, spread, preferred_element_type=F32)

    spots_all = (regroup(z_high) * 64.0 + regroup(z_low)).astype(I32)
    for c in range(local_clusters):
        tpos[c] = spots_all[c : c + 1, :]

    item_wide = iota((item_rows, seats), 0)
    low_wide = iota((LANES, seats), 0)
    high_wide = iota((groups, seats), 0)
    loss_lane = iota((1, loss_out.shape[1]), 1)
    together = 4

    def look_up(c):
        spot = tpos[c] - 1
        live = spot >= 0
        near = jnp.dot(
            lookup[c].astype(BF16),
            flags((spot & (LANES - 1)) == low_wide),
            preferred_element_type=F32,
        )
        here = lax.shift_right_logical(spot, log2(LANES)) == high_wide
        found = [
            jnp.sum(
                jnp.where(here, near[n * groups : (n + 1) * groups, :], 0.0), axis=0, keepdims=True
            )
            for n in range(3)
        ]
        own_item[c] = jnp.where(live, found[0], -1.0).astype(I32)
        own_count[c] = jnp.log(jnp.where(live, found[1] * 64.0 + found[2], 1.0))

    def look_up_some(n):
        for u in range(together):
            look_up(n * together + u)

    each(0, local_clusters // together, look_up_some)

    for j in range(line):
        each(1, plane, lambda i: seat_copy(j, i).wait_recv())

    def own(c, losses):
        query = got[c].reshape(seats, width)
        block = items[c]
        scores = lax.dot_general(
            block, query, (((1,), (1,)), ((), ())), preferred_element_type=F32
        )
        shifted = scores + mass[c]
        top = jnp.max(shifted, axis=0, keepdims=True)
        expo = jnp.exp(shifted - top)
        total = jnp.sum(expo, axis=0, keepdims=True)
        mine = own_item[c]
        live = jnp.where(mine >= 0, 1.0, 0.0)
        hit = mine == item_wide
        picked = jnp.sum(jnp.where(hit, scores, 0.0), axis=0, keepdims=True) - own_count[c]
        loss = (jnp.log(total) + top - picked) * live
        mean = jnp.sum(loss, axis=1, keepdims=True) / jnp.sum(live, axis=1, keepdims=True)
        weight = (expo * (1.0 / total) - jnp.where(hit, 1.0, 0.0)).astype(BF16)
        wts[c] = weight
        dq = lax.dot_general(weight, block, (((0,), (0,)), ((), ())), preferred_element_type=F32)
        dqs[c] = dq.reshape(line * plane, cap, width).astype(BF16)
        return jnp.where(loss_lane == c, mean, losses)

    def own_some(n, losses):
        for u in range(together):
            losses = own(n * together + u, losses)
        return losses

    loss_out[...] = lax.fori_loop(
        0, local_clusters // together, own_some, jnp.zeros(loss_out.shape, F32)
    )

    for j in range(line - 1, -1, -1):
        each(1, plane, lambda i: back_copy(j, i).start())
        ret[j, 0] = dqs[:, j * plane]

    def tables(c):
        table_out[c] = jnp.dot(
            wts[c], got[c].reshape(seats, width), preferred_element_type=F32
        )

    each(0, local_clusters, tables)

    def gather(j):
        each(1, plane, lambda i: back_copy(j, i).wait_recv())
        return lax.dot_general(
            sel[j].reshape(plane * rows, users),
            ret[j].reshape(plane * rows, width),
            (((0,), (0,)), ((), ())),
            preferred_element_type=F32,
        )

    def push(j, value):
        pstage[j] = value.astype(BF16)
        for h in range(2):
            part_copy(j, h).start()

    push(3, gather(3))
    second = gather(2)
    for h in range(2):
        span = slice(h * piece, (h + 1) * piece)
        part_copy(3, h).wait_recv()
        pstage[2, span, :] = (second[span, :] + part[3, span, :].astype(F32)).astype(BF16)
        part_copy(2, h).start()
    push(1, gather(1))
    total = gather(0)
    for j in (1, 2):
        for h in range(2):
            part_copy(j, h).wait_recv()
        total = total + part[j].astype(F32)
    dq_total = total.astype(BF16)

    feat, hid = features.shape[1], hidden.shape[1]
    dhidden = lax.dot_general(
        dq_total, w_out[...], (((1,), (1,)), ((), ())), preferred_element_type=F32
    )
    dpre = (dhidden * slope[...]).astype(BF16)
    wide = 2 * LANES
    for b in range(hid // wide):
        product = jnp.dot(
            features_t[...], dpre[:, b * wide : (b + 1) * wide], preferred_element_type=F32
        )
        for h in range(2):
            acc[(2 * b + h) * feat : (2 * b + h + 1) * feat, :] = product[
                :, h * LANES : (h + 1) * LANES
            ]
    big_rows = feat * (hid // LANES)
    acc[big_rows : big_rows + hid, :] = lax.dot_general(
        hidden[...], dq_total, (((0,), (0,)), ((), ())), preferred_element_type=F32
    )
    if acc.shape[0] > big_rows + hid:
        spare = acc.shape[0] - big_rows - hid
        acc[big_rows + hid :, :] = jnp.zeros((spare, LANES), F32)

    chips = plane // 2
    core, chip = p % 2, p // 2
    cuts, half = summed_groups(line, chips, (feat + width) * hid)
    base = core * half
    away = (1 - core) * half

    def at(start, size):
        return pl.ds(pl.multiple_of(start, TILE), size)

    class Cut:
        def __init__(self, n):
            self.n = n
            self.plane_first, self.start, self.size = cuts[n]
            self.count1, self.count2 = (chips, line) if self.plane_first else (line, chips)
            self.size1 = self.size // self.count1
            self.size2 = self.size1 // self.count2
            self.in1, self.in2 = inboxes[2 * n], inboxes[2 * n + 1]

        def device1(self, i):
            return inside(2 * i) if self.plane_first else along(i)

        def device2(self, i):
            return along(i) if self.plane_first else inside(2 * i)

        def block(self, i):
            mine = chip if self.plane_first else z
            return base + self.start + flip(mine, i, self.count1) * self.size1

        def piece(self, i, j):
            mine = z if self.plane_first else chip
            return self.block(i) + flip(mine, j, self.count2) * self.size2

    cut = [Cut(n) for n in range(len(cuts))]
    started = []

    def give(start, size, inbox, sems, index, device):
        span = at(start, size)
        outb[span, :] = acc[span, :].astype(BF16)
        copy = remote(outb.at[span, :], inbox, sems, index, device)
        copy.start()
        started.append(copy)
        return copy

    def added(start, size, arrived):
        total = acc[at(start, size), :]
        for inbox in arrived:
            total = total + inbox.astype(F32)
        return total

    def share(start, size, sems, index, device):
        span = at(start, size)
        copy = remote(full.at[span, :], full.at[span, :], sems, index, device)
        copy.start()
        started.append(copy)
        return copy

    def finish(copies):
        for copy in copies:
            copy.wait_recv()

    first = [
        give(away + c.start, c.size, core_in.at[c.start : c.start + c.size, :], c_sem, (c.n,), inside(1))
        for c in cut
    ]
    second = []
    for c in cut:
        first[c.n].wait_recv()
        mine = base + c.start
        acc[at(mine, c.size), :] = added(mine, c.size, [core_in[c.start : c.start + c.size, :]])
        second.append(
            [
                give(c.block(i), c.size1, c.in1.at[i], s1_sem, (c.n, i), c.device1(i))
                for i in range(1, c.count1)
            ]
        )
    third = []
    for c in cut:
        finish(second[c.n])
        acc[at(c.block(0), c.size1), :] = added(
            c.block(0), c.size1, [c.in1[i] for i in range(1, c.count1)]
        )
        third.append(
            [
                give(c.piece(0, j), c.size2, c.in2.at[j], s2_sem, (c.n, j), c.device2(j))
                for j in range(1, c.count2)
            ]
        )
    outer, inner, last = {}, {}, []
    for c in cut:
        finish(third[c.n])
        mine = c.piece(0, 0)
        full[at(mine, c.size2), :] = added(
            mine, c.size2, [c.in2[j] for j in range(1, c.count2)]
        ).astype(BF16)
        for j in range(1, c.count2):
            inner[c.n, j] = share(mine, c.size2, g2_sem, (c.n, j), c.device2(j))
        for i in range(1, c.count1):
            outer[c.n, i, 0] = share(mine, c.size2, g1_sem, (c.n, i, 0), c.device1(i))
    for c in cut:
        for j in range(1, c.count2):
            inner[c.n, j].wait_recv()
            for i in range(1, c.count1):
                outer[c.n, i, j] = share(
                    c.piece(0, j), c.size2, g1_sem, (c.n, i, j), c.device1(i)
                )
        last.append(share(c.block(0), c.size1, go_sem, (c.n, 0), inside(1)))
    for c in cut:
        for i in range(1, c.count1):
            finish(outer[c.n, i, j] for j in range(c.count2))
            last.append(share(c.block(i), c.size1, go_sem, (c.n, i), inside(1)))
    finish(last)
    for b in range(hid // LANES):
        big_out[:, b * LANES : (b + 1) * LANES] = full[b * feat : (b + 1) * feat, :].astype(
            big_out.dtype
        )
    small_out[...] = full[big_rows : big_rows + hid, :].astype(small_out.dtype)

    for copy in started:
        copy.wait_send()
    for j in range(1, line):
        for copy in meta_copies(j):
            copy.wait_send()
        for h in range(2):
            query_copy(j, h).wait_send()
            part_copy(j, h).wait_send()

    def sent(i):
        target_copy(i).wait_send()
        for j in range(line):
            seat_copy(j, i).wait_send()
            back_copy(j, i).wait_send()

    each(1, plane, sent)


def local(
    features, w_hidden, w_out, items, routes, cluster_slot, sample_ids, sample_counts, positives
):
    devices = lax.axis_size("dev")
    line, plane = LINE, devices // LINE
    chips = plane // 2
    users, visits = routes.shape
    feat, hid = w_hidden.shape
    width = w_out.shape[1]
    clusters = cluster_slot.shape[0]
    local_clusters, samples = sample_ids.shape
    item_rows = items.shape[0] // local_clusters
    cap = max(2, 2 * users * visits // (local_clusters * devices))
    rows = local_clusters * cap
    hosted = plane * local_clusters
    seats = devices * cap
    groups = samples // LANES
    cuts, half = summed_groups(line, chips, (feat + width) * hid)
    most = max(chips, line)
    inboxes = []
    for plane_first, _, size in cuts:
        count1, count2 = (chips, line) if plane_first else (line, chips)
        inboxes.append(pltpu.VMEM((count1, size // count1, LANES), BF16))
        inboxes.append(pltpu.VMEM((count2, size // count1 // count2, LANES), BF16))
    vmem = pl.BlockSpec(memory_space=pltpu.VMEM)
    hbm = pl.BlockSpec(memory_space=pltpu.HBM)
    dma = pltpu.SemaphoreType.DMA
    loss, big, small, table = pl.pallas_call(
        functools.partial(step_kernel, line, plane, cap),
        out_shape=(
            jax.ShapeDtypeStruct((1, local_clusters), F32),
            jax.ShapeDtypeStruct((feat, hid), OUT),
            jax.ShapeDtypeStruct((hid, width), OUT),
            jax.ShapeDtypeStruct((local_clusters, item_rows, width), F32),
        ),
        in_specs=[hbm] * 9,
        out_specs=[vmem] * 4,
        scratch_shapes=[
            pltpu.VMEM((users, feat), BF16),
            pltpu.VMEM((feat, users), BF16),
            pltpu.VMEM((feat, hid), BF16),
            pltpu.VMEM((hid, width), BF16),
            pltpu.VMEM((local_clusters, item_rows, width), BF16),
            pltpu.VMEM((local_clusters, samples), I32),
            pltpu.VMEM((local_clusters, samples), I32),
            pltpu.VMEM((visits, users), I32),
            pltpu.VMEM((visits, users), I32),
            pltpu.VMEM((1, clusters), I32),
            pltpu.VMEM((users, hid), F32),
            pltpu.VMEM((users, hid), BF16),
            pltpu.VMEM((2, line, visits, users), I32),
            pltpu.VMEM((line, users, width), BF16),
            pltpu.VMEM((users, users), BF16),
            pltpu.VMEM((hosted, users), F32),
            pltpu.VMEM((line, plane, rows, users), BF16),
            pltpu.VMEM((line, plane, local_clusters, cap, width), BF16),
            pltpu.VMEM((local_clusters, devices, cap, width), BF16),
            pltpu.VMEM((plane, local_clusters, LANES), F32),
            pltpu.VMEM((plane, local_clusters, LANES), F32),
            pltpu.VMEM((local_clusters, 3 * groups, LANES), F32),
            pltpu.VMEM((3 * local_clusters * (item_rows // 16), min(1024, samples)), BF16),
            pltpu.VMEM((16 * local_clusters, min(1024, samples)), BF16),
            pltpu.VMEM((3 * local_clusters * (item_rows // 16), 16 * local_clusters), F32),
            pltpu.VMEM((local_clusters, item_rows, 1), F32),
            pltpu.VMEM((local_clusters, 1, seats), I32),
            pltpu.VMEM((local_clusters, 1, seats), I32),
            pltpu.VMEM((local_clusters, 1, seats), F32),
            pltpu.VMEM((local_clusters, item_rows, seats), BF16),
            pltpu.VMEM((local_clusters, devices, cap, width), BF16),
            pltpu.VMEM((line, plane, local_clusters, cap, width), BF16),
            pltpu.VMEM((line, users, width), BF16),
            pltpu.VMEM((line, users, width), BF16),
            pltpu.VMEM((2 * half, LANES), F32),
            pltpu.VMEM((2 * half, LANES), BF16),
            pltpu.VMEM((half, LANES), BF16),
            inboxes,
            pltpu.VMEM((2 * half, LANES), BF16),
            dma((10,)),
            dma((2, 2, line)),
            dma((2, line, 2)),
            dma((2, line, plane)),
            dma((2, plane)),
            dma((2, line, plane)),
            dma((2, line, 2)),
            dma((2, len(cuts))),
            dma((2, len(cuts), most)),
            dma((2, len(cuts), most)),
            dma((2, len(cuts), most, most)),
            dma((2, len(cuts), most)),
            dma((2, len(cuts), most)),
        ],
        compiler_params=pltpu.CompilerParams(
            collective_id=0, has_side_effects=True, vmem_limit_bytes=VMEM_BYTES
        ),
        name="step",
    )(
        *(
            pltpu.with_memory_space_constraint(array, pltpu.HBM)
            for array in (
                features,
                w_hidden,
                w_out,
                items.reshape(local_clusters, item_rows, width),
                sample_ids,
                sample_counts,
                routes.T,
                positives.T,
                cluster_slot.reshape(1, clusters),
            )
        )
    )
    return finish(loss, big, small, table.reshape(items.shape))


def finish_kernel(loss_ref, big_ref, small_ref, table_ref, loss_out, big_out, small_out, table_out):
    loss_out[...] = loss_ref[...].reshape(loss_out.shape)
    big_out[...] = big_ref[...].astype(F32)
    small_out[...] = small_ref[...].astype(F32)
    table_out[...] = table_ref[...]


def finish(loss, big, small, table):
    steps = 4

    def cut(array):
        shape = array.shape
        return pl.BlockSpec((shape[0] // steps, shape[1]), lambda n: (n, 0))

    specs = [cut(big), cut(small), cut(table)]
    return pl.pallas_call(
        finish_kernel,
        grid=(steps,),
        out_shape=(
            jax.ShapeDtypeStruct(loss.shape[1:], F32),
            jax.ShapeDtypeStruct(big.shape, F32),
            jax.ShapeDtypeStruct(small.shape, F32),
            jax.ShapeDtypeStruct(table.shape, F32),
        ),
        in_specs=[pl.BlockSpec(loss.shape, lambda n: (0, 0))] + specs,
        out_specs=[pl.BlockSpec(loss.shape[1:], lambda n: (0,))] + specs,
        compiler_params=pltpu.CompilerParams(vmem_limit_bytes=VMEM_BYTES),
        name="finish",
    )(loss, big, small, table)


OUT = BF16


def solution(mesh):
    in_specs = (
        P("dev", None),
        P(),
        P(),
        P("dev", None),
        P("dev", None),
        P(),
        P("dev", None),
        P("dev", None),
        P("dev", None),
    )
    out_specs = (P("dev"), P(), P(), P("dev", None))
    return jax.shard_map(local, mesh=mesh, in_specs=in_specs, out_specs=out_specs, check_vma=False)
```

profile of v0, /device:TPU:1, one launch (start us, length us, event | category | flops | bytes accessed | tf_op | source)
XLA Modules:
  0.0 80.5 jit_solution(12911470337510482603)
XLA Ops:
  0.6 77.6 %step.1 = (f32[1,16]{1,0:T(1,128)S(1)}, bf16[1024,512]{1,0:T(8,128)(2,1)S(1)}, bf16[512,128]{1,0:T(8,128)(2,1)S(1)}, f32[16,128,128]{2,1,0:T(8,128)S(1)}) custom-call(bf16[512,1024]{1,0:T(8,128)(2,1)} %features_hbm.1, bf16[1024,512]{1,0:T(8,128)(2,1)} %w_hidden_hbm.1, bf16[512,128]{1,0:T(8,128)(2,1)} %w_out_hbm.1, bf16[16,128,128]{2,1,0:T(8,128)(2,1)} %bitcast.6, ...), custom_call_target="tpu_custom_call" | custom-call | tf_op jit(solution)/shard_map/step/pallas_call | solution.py:720
  78.2 2.2 %finish.1 = (f32[16]{0:T(128)}, f32[1024,512]{1,0:T(8,128)}, f32[512,128]{1,0:T(8,128)}, f32[2048,128]{1,0:T(8,128)}) custom-call(f32[1,16]{1,0:T(1,128)S(1)} %get-tuple-element.8.loss_ref, bf16[1024,512]{1,0:T(8,128)(2,1)S(1)} %get-tuple-element.9.big_ref, bf16[512,128]{1,0:T(8,128)(2,1)S(1)} %get-tuple-element.10.small_ref, f32[2048,128]{1,0:T(8,128)S(1)} %bitcast.5), custom_call_target="tpu_custom_call" | custom-call | tf_op jit(solution)/shard_map/finish/pallas_call | solution.py:822
where the time goes:
time: 80.6 us; the launch traced here: 80.5 us
  Pallas kernels  79.8 us (99%)
    pallas_call x1, Pallas kernels, local(): pl.pallas_call(functools.partial(step_kernel, line, plane, cap), out_shap...  77.6 us
    pallas_call x1, Pallas kernels, finish(): pl.pallas_call(finish_kernel, grid=(steps,), out_shape=(jax.ShapeDtypeStr...  2.23 us

commit v1 on v0

--- a/solution.py
+++ b/solution.py
@@ -64,7 +64,7 @@
     groups = []
     start = 0
     for n in range(pieces):
-        plane_first, share = True, (units + pieces - 1 - n) // pieces
+        plane_first, share = n % 2 == 0, (units + pieces - 1 - n) // pieces
         if share > 0:
             groups.append((plane_first, start, share * parts))
             start += share * parts
@@ -214,8 +214,16 @@
     def target_copy(i):
         return remote(zstage.at[i], zgot.at[i], t_sem, (i,), inside(i))
 
-    def back_copy(j, i):
-        return remote(dqs.at[:, j * plane + i], ret.at[j, i], r_sem, (j, i), inside(i))
+    own_half = local_clusters // 2
+
+    def back_copy(j, i, g):
+        some = pl.ds(g * own_half, own_half)
+        return remote(
+            dqs.at[some, j * plane + i], ret.at[j, i, some], r_sem, (j, i, g), inside(i)
+        )
+
+    def back_copies(j, g):
+        each(1, plane, lambda i: back_copy(j, i, g).start())
 
     def part_copy(j, h):
         return half_copy(pstage, part, p_sem, j, h, j, along(1 if j == 3 else j))
@@ -233,6 +241,7 @@
         slope[span, :] = pre
         qline[0, span, :] = jnp.dot(active, w_out[...], preferred_element_type=F32).astype(BF16)
         query_copy(2, h).start()
+    for h in range(2):
         query_copy(1, h).start()
 
     for load in loads[4:6]:
@@ -489,12 +498,19 @@
             losses = own(n * together + u, losses)
         return losses
 
+    losses = lax.fori_loop(0, own_half // together, own_some, jnp.zeros(loss_out.shape, F32))
+    for j in (3, 2):
+        back_copies(j, 0)
     loss_out[...] = lax.fori_loop(
-        0, local_clusters // together, own_some, jnp.zeros(loss_out.shape, F32)
+        own_half // together, local_clusters // together, own_some, losses
     )
+    for j in (3, 2):
+        back_copies(j, 1)
+    for j in (1, 0):
+        for g in range(2):
+            back_copies(j, g)
 
     for j in range(line - 1, -1, -1):
-        each(1, plane, lambda i: back_copy(j, i).start())
         ret[j, 0] = dqs[:, j * plane]
 
     def tables(c):
@@ -505,7 +521,8 @@
     each(0, local_clusters, tables)
 
     def gather(j):
-        each(1, plane, lambda i: back_copy(j, i).wait_recv())
+        for g in range(2):
+            each(1, plane, lambda i: back_copy(j, i, g).wait_recv())
         return lax.dot_general(
             sel[j].reshape(plane * rows, users),
             ret[j].reshape(plane * rows, width),
@@ -685,7 +702,8 @@
         target_copy(i).wait_send()
         for j in range(line):
             seat_copy(j, i).wait_send()
-            back_copy(j, i).wait_send()
+            for g in range(2):
+                back_copy(j, i, g).wait_send()
 
     each(1, plane, sent)
 
@@ -772,7 +790,7 @@
             dma((2, line, 2)),
             dma((2, line, plane)),
             dma((2, plane)),
-            dma((2, line, plane)),
+            dma((2, line, plane, 2)),
             dma((2, line, 2)),
             dma((2, len(cuts))),
             dma((2, len(cuts), most)),

time: 80.6 us -> 77.6 us (0.963)
  Pallas kernels: 79.8 us -> 76.8 us
    pallas_call x1, Pallas kernels: 77.6 us -> 74.6 us  [local(): pl.pallas_call(functools.partial(step_kernel, line, plane, cap), out_shap...]
where the time goes in v1:
time: 77.6 us; the launch traced here: 77.5 us
  Pallas kernels  76.8 us (99%)
    pallas_call x1, Pallas kernels, local(): pl.pallas_call(functools.partial(step_kernel, line, plane, cap), out_shap...  74.6 us
    pallas_call x1, Pallas kernels, finish(): pl.pallas_call(finish_kernel, grid=(steps,), out_shape=(jax.ShapeDtypeStr...  2.23 us

profile of v1, /device:TPU:1, one launch (start us, length us, event | category | flops | bytes accessed | tf_op | source)
XLA Modules:
  0.0 77.5 jit_solution(14458614835695619080)
XLA Ops:
  0.6 74.6 %step.1 = (f32[1,16]{1,0:T(1,128)S(1)}, bf16[1024,512]{1,0:T(8,128)(2,1)S(1)}, bf16[512,128]{1,0:T(8,128)(2,1)S(1)}, f32[16,128,128]{2,1,0:T(8,128)S(1)}) custom-call(bf16[512,1024]{1,0:T(8,128)(2,1)} %features_hbm.1, bf16[1024,512]{1,0:T(8,128)(2,1)} %w_hidden_hbm.1, bf16[512,128]{1,0:T(8,128)(2,1)} %w_out_hbm.1, bf16[16,128,128]{2,1,0:T(8,128)(2,1)} %bitcast.6, ...), custom_call_target="tpu_custom_call" | custom-call | tf_op jit(solution)/shard_map/step/pallas_call | solution.py:738
  75.2 2.2 %finish.1 = (f32[16]{0:T(128)}, f32[1024,512]{1,0:T(8,128)}, f32[512,128]{1,0:T(8,128)}, f32[2048,128]{1,0:T(8,128)}) custom-call(f32[1,16]{1,0:T(1,128)S(1)} %get-tuple-element.8.loss_ref, bf16[1024,512]{1,0:T(8,128)(2,1)S(1)} %get-tuple-element.9.big_ref, bf16[512,128]{1,0:T(8,128)(2,1)S(1)} %get-tuple-element.10.small_ref, f32[2048,128]{1,0:T(8,128)S(1)} %bitcast.5), custom_call_target="tpu_custom_call" | custom-call | tf_op jit(solution)/shard_map/finish/pallas_call | solution.py:840

commit v2 on v1

--- a/solution.py
+++ b/solution.py
@@ -208,13 +208,16 @@
         source, device = (2, along(1)) if j == 3 else (0, along(j))
         return half_copy(qline, qline, q_sem, j, h, source, device)
 
-    def seat_copy(j, i):
-        return remote(stage.at[j, i], got.at[:, j * plane + i], x_sem, (j, i), inside(i))
+    own_half = local_clusters // 2
+
+    def seat_copy(j, i, g):
+        some = pl.ds(g * own_half, own_half)
+        return remote(
+            stage.at[j, i, some], got.at[some, j * plane + i], x_sem, (j, i, g), inside(i)
+        )
 
     def target_copy(i):
         return remote(zstage.at[i], zgot.at[i], t_sem, (i,), inside(i))
-
-    own_half = local_clusters // 2
 
     def back_copy(j, i, g):
         some = pl.ds(g * own_half, own_half)
@@ -303,9 +306,13 @@
     def send_seats(j):
         def block(i):
             stage[j, i] = seated(j, i)
-            seat_copy(j, i).start()
+            seat_copy(j, i, 0).start()
+            if j < line - 1:
+                seat_copy(j, i, 1).start()
 
         each(1, plane, block)
+        if j == line - 1:
+            each(1, plane, lambda i: seat_copy(j, i, 1).start())
         got[:, j * plane] = seated(j, 0)
 
     def relay():
@@ -469,7 +476,8 @@
     each(0, local_clusters // together, look_up_some)
 
     for j in range(line):
-        each(1, plane, lambda i: seat_copy(j, i).wait_recv())
+        for g in range(1 if j == line - 1 else 2):
+            each(1, plane, lambda i: seat_copy(j, i, g).wait_recv())
 
     def own(c, losses):
         query = got[c].reshape(seats, width)
@@ -501,6 +509,7 @@
     losses = lax.fori_loop(0, own_half // together, own_some, jnp.zeros(loss_out.shape, F32))
     for j in (3, 2):
         back_copies(j, 0)
+    each(1, plane, lambda i: seat_copy(line - 1, i, 1).wait_recv())
     loss_out[...] = lax.fori_loop(
         own_half // together, local_clusters // together, own_some, losses
     )
@@ -519,6 +528,20 @@
         )
 
     each(0, local_clusters, tables)
+
+    for j in range(1, line):
+        for copy in meta_copies(j):
+            copy.wait_send()
+        for h in range(2):
+            query_copy(j, h).wait_send()
+
+    def forward_sent(i):
+        target_copy(i).wait_send()
+        for j in range(line):
+            for g in range(2):
+                seat_copy(j, i, g).wait_send()
+
+    each(1, plane, forward_sent)
 
     def gather(j):
         for g in range(2):
@@ -636,6 +659,17 @@
         give(away + c.start, c.size, core_in.at[c.start : c.start + c.size, :], c_sem, (c.n,), inside(1))
         for c in cut
     ]
+
+    def backward_sent(i):
+        for j in range(line):
+            for g in range(2):
+                back_copy(j, i, g).wait_send()
+
+    each(1, plane, backward_sent)
+    for j in range(1, line):
+        for h in range(2):
+            part_copy(j, h).wait_send()
+
     second = []
     for c in cut:
         first[c.n].wait_recv()
@@ -691,21 +725,6 @@
 
     for copy in started:
         copy.wait_send()
-    for j in range(1, line):
-        for copy in meta_copies(j):
-            copy.wait_send()
-        for h in range(2):
-            query_copy(j, h).wait_send()
-            part_copy(j, h).wait_send()
-
-    def sent(i):
-        target_copy(i).wait_send()
-        for j in range(line):
-            seat_copy(j, i).wait_send()
-            for g in range(2):
-                back_copy(j, i, g).wait_send()
-
-    each(1, plane, sent)
 
 
 def local(
@@ -788,7 +807,7 @@
             dma((10,)),
             dma((2, 2, line)),
             dma((2, line, 2)),
-            dma((2, line, plane)),
+            dma((2, line, plane, 2)),
             dma((2, plane)),
             dma((2, line, plane, 2)),
             dma((2, line, 2)),
@@ -830,7 +849,7 @@
 
 
 def finish(loss, big, small, table):
-    steps = 4
+    steps = 2
 
     def cut(array):
         shape = array.shape

time: 77.6 us -> 77.3 us (level)
  no operation moved by 1% of the time
where the time goes in v2:
time: 77.3 us; the launch traced here: 77.2 us
  Pallas kernels  76.5 us (99%)
    pallas_call x1, Pallas kernels, local(): pl.pallas_call(functools.partial(step_kernel, line, plane, cap), out_shap...  74.6 us
    pallas_call x1, Pallas kernels, finish(): pl.pallas_call(finish_kernel, grid=(steps,), out_shape=(jax.ShapeDtypeStr...  1.9 us

profile of v2, /device:TPU:1, one launch (start us, length us, event | category | flops | bytes accessed | tf_op | source)
XLA Modules:
  0.0 77.2 jit_solution(16955526395233059994)
XLA Ops:
  0.6 74.6 %step.1 = (f32[1,16]{1,0:T(1,128)S(1)}, bf16[1024,512]{1,0:T(8,128)(2,1)S(1)}, bf16[512,128]{1,0:T(8,128)(2,1)S(1)}, f32[16,128,128]{2,1,0:T(8,128)S(1)}) custom-call(bf16[512,1024]{1,0:T(8,128)(2,1)} %features_hbm.1, bf16[1024,512]{1,0:T(8,128)(2,1)} %w_hidden_hbm.1, bf16[512,128]{1,0:T(8,128)(2,1)} %w_out_hbm.1, bf16[16,128,128]{2,1,0:T(8,128)(2,1)} %bitcast.6, ...), custom_call_target="tpu_custom_call" | custom-call | tf_op jit(solution)/shard_map/step/pallas_call | solution.py:757
  75.3 1.9 %finish.1 = (f32[16]{0:T(128)}, f32[1024,512]{1,0:T(8,128)}, f32[512,128]{1,0:T(8,128)}, f32[2048,128]{1,0:T(8,128)}) custom-call(f32[1,16]{1,0:T(1,128)S(1)} %get-tuple-element.8.loss_ref, bf16[1024,512]{1,0:T(8,128)(2,1)S(1)} %get-tuple-element.9.big_ref, bf16[512,128]{1,0:T(8,128)(2,1)S(1)} %get-tuple-element.10.small_ref, f32[2048,128]{1,0:T(8,128)S(1)} %bitcast.5), custom_call_target="tpu_custom_call" | custom-call | tf_op jit(solution)/shard_map/finish/pallas_call | solution.py:859

commit v3 on v2

--- a/solution.py
+++ b/solution.py
@@ -407,11 +407,10 @@
             mass[c] = logs[:, c : c + 1]
 
     chunks = samples // chunk
-    each(0, chunks // 2, weigh)
+    each(0, chunks, weigh)
     for h in range(2):
         query_copy(3, h).wait_recv()
     send_seats(3)
-    each(chunks // 2, chunks, weigh)
     settle_masses()
     pre = slope[...]
     gate = 1.0 / (1.0 + jnp.exp(-pre))

time: 77.3 us -> 77.2 us (level)
  no operation moved by 1% of the time
where the time goes in v3:
time: 77.2 us; the launch traced here: 77 us
  Pallas kernels  76.4 us (99%)
    pallas_call x1, Pallas kernels, local(): pl.pallas_call(functools.partial(step_kernel, line, plane, cap), out_shap...  74.5 us
    pallas_call x1, Pallas kernels, finish(): pl.pallas_call(finish_kernel, grid=(steps,), out_shape=(jax.ShapeDtypeStr...  1.9 us

profile of v3, /device:TPU:1, one launch (start us, length us, event | category | flops | bytes accessed | tf_op | source)
XLA Modules:
  0.0 77.0 jit_solution(18317321721935609303)
XLA Ops:
  0.6 74.5 %step.1 = (f32[1,16]{1,0:T(1,128)S(1)}, bf16[1024,512]{1,0:T(8,128)(2,1)S(1)}, bf16[512,128]{1,0:T(8,128)(2,1)S(1)}, f32[16,128,128]{2,1,0:T(8,128)S(1)}) custom-call(bf16[512,1024]{1,0:T(8,128)(2,1)} %features_hbm.1, bf16[1024,512]{1,0:T(8,128)(2,1)} %w_hidden_hbm.1, bf16[512,128]{1,0:T(8,128)(2,1)} %w_out_hbm.1, bf16[16,128,128]{2,1,0:T(8,128)(2,1)} %bitcast.6, ...), custom_call_target="tpu_custom_call" | custom-call | tf_op jit(solution)/shard_map/step/pallas_call | solution.py:756
  75.1 1.9 %finish.1 = (f32[16]{0:T(128)}, f32[1024,512]{1,0:T(8,128)}, f32[512,128]{1,0:T(8,128)}, f32[2048,128]{1,0:T(8,128)}) custom-call(f32[1,16]{1,0:T(1,128)S(1)} %get-tuple-element.8.loss_ref, bf16[1024,512]{1,0:T(8,128)(2,1)S(1)} %get-tuple-element.9.big_ref, bf16[512,128]{1,0:T(8,128)(2,1)S(1)} %get-tuple-element.10.small_ref, f32[2048,128]{1,0:T(8,128)S(1)} %bitcast.5), custom_call_target="tpu_custom_call" | custom-call | tf_op jit(solution)/shard_map/finish/pallas_call | solution.py:858
